TPU v7x, 256 devices: a whole 4x4x8 slice. The times are simulated.
256 devices in a mesh: dp: 16 (over y_lo, x, core), chan: 16 (over y_hi, z).
Axes of the slice: x: 4, y: 4 (y_hi: 2, y_lo: 2; y = y_hi * 2 + y_lo), z: 8, core: 2. Of those that a mesh axis runs over, the one named last changes fastest.
Arguments:
- anchors: bfloat16 [256, 128, 4096], P('dp', 'chan'), may hold values from -15 to 15
- views: bfloat16 [256, 128, 4096], P('dp', 'chan'), may hold values from -15 to 15
- dw_weight: float32 [128, 4], replicated, may hold values from -3 to 3
- pw_weight: bfloat16 [256, 128], replicated, may hold values from -0.5 to 0.5
- proj_weight: bfloat16 [256, 1024], replicated, may hold values from -0.375 to 0.375
- partner: int32 [256], P('dp'), may hold values from 0 to 255, each once
Outputs:
- loss: float32 [256], P('dp')
- grad_dw: float32 [128, 4], P('chan')
- grad_pw: float32 [256, 128], replicated
- grad_proj: float32 [256, 1024], P('chan', 'dp')
Inputs may be any that keep to these rules, and one draw needn't show every extreme that they name: `partner`: each view index appears exactly once.
All inputs are finite; a program needn't handle non-finite values.
Results may differ from a plain program's by a relative error of at most 0.0044.
Values may be sent and summed in bfloat16 or wider, within the bound.
No kernel may reach another device: no remote copies, remote signals or barrier semaphores. Data moves between devices by JAX's collectives and lax.ppermute only.
A program may use at most 192 MiB of HBM per device.

v0:
```python
import jax
import jax.numpy as jnp
from jax import lax
from jax.sharding import PartitionSpec as P

TAPS = 4
TAP_SPACING = 16
logit_scale = 16.0


def passed_along(value, axis, steps):
    count = lax.axis_size(axis)
    pairs = [(source, (source + steps) % count) for source in range(count)]
    return lax.ppermute(value, axis, pairs)


def depthwise(trace_block, dw_weight):
    widened = trace_block.astype(jnp.float32)
    length = trace_block.shape[2]
    running = jnp.zeros(widened.shape, jnp.float32)
    for tap_index in range(TAPS):
        offset_steps = tap_index * TAP_SPACING
        shifted = jnp.pad(
            widened[:, :, : length - offset_steps], ((0, 0), (0, 0), (offset_steps, 0))
        )
        running = running + dw_weight[None, :, tap_index, None] * shifted
    return running.astype(jnp.bfloat16)


def silu_slope(mixed):
    sigma = jax.nn.sigmoid(mixed)
    return sigma * (1.0 + mixed * (1.0 - sigma))


def kernel_terms(grad_conv, extended):
    rim_width = (TAPS - 1) * TAP_SPACING
    span_width = grad_conv.shape[2]
    columns = []
    for tap_index in range(TAPS):
        begin = rim_width - tap_index * TAP_SPACING
        window = extended[:, :, begin : begin + span_width]
        columns.append(
            jnp.einsum("nct,nct->c", grad_conv, window, preferred_element_type=jnp.float32)
        )
    return jnp.stack(columns, 1)


def block_scores(queries, key_rows, owner_index, partner, factor):
    logits = factor * lax.dot_general(
        queries, key_rows, (((1,), (1,)), ((), ())), preferred_element_type=jnp.float32
    )
    columns = owner_index * key_rows.shape[0] + jnp.arange(key_rows.shape[0], dtype=jnp.int32)
    matches = columns[None, :] == partner[:, None]
    return (logits, matches)


def body(anchors, views, dw_weight, pw_weight, proj_weight, partner):
    stacked = jnp.concatenate([anchors, views], 0)
    pair_count = anchors.shape[0]
    length = anchors.shape[2]
    chan_index = lax.axis_index("chan")
    chan_count = lax.axis_size("chan")
    cycle_index = lax.axis_index("dp")
    cycle_size = lax.axis_size("dp")
    rim_width = (TAPS - 1) * TAP_SPACING
    local_metrics = anchors.shape[1]
    local_kernel = lax.dynamic_slice_in_dim(dw_weight, chan_index * local_metrics, local_metrics, 0)
    conv_local = depthwise(stacked, local_kernel)
    conv_rows = lax.all_to_all(conv_local, "chan", split_axis=2, concat_axis=1, tiled=True)
    mixed = jnp.einsum("fc,nct->nft", pw_weight, conv_rows, preferred_element_type=jnp.float32)
    partial_pool = jnp.sum(jax.nn.silu(mixed), 2) / length
    conv_time, mixed, partial_pool = (conv_rows, mixed, partial_pool)
    pooled = lax.psum(partial_pool, "chan")
    pooled_bf = pooled.astype(jnp.bfloat16)
    embedding = jnp.dot(pooled_bf, proj_weight, preferred_element_type=jnp.float32)
    inverse = lax.rsqrt(jnp.mean(embedding * embedding, 1, keepdims=True) + 1e-06)
    unit_rows = embedding * inverse
    unit_bf = unit_rows.astype(jnp.bfloat16)
    queries = unit_bf[:pair_count]
    own_keys = unit_bf[pair_count:]
    factor = logit_scale / proj_weight.shape[1]

    def total_terms(key_rows, owner_index, totals, positive):
        logits, matches = block_scores(queries, key_rows, owner_index, partner, factor)
        totals = totals + jnp.sum(jnp.exp(logits - logit_scale), 1)
        positive = positive + jnp.sum(jnp.where(matches, logits, 0.0), 1)
        return (totals, positive)

    def first_turn(turn_index, loop_state):
        key_rows, totals, positive = loop_state
        owner_index = (cycle_index - turn_index) % cycle_size
        totals, positive = total_terms(key_rows, owner_index, totals, positive)
        key_rows = passed_along(key_rows, "dp", 1)
        return (key_rows, totals, positive)

    start_zero = jnp.zeros((pair_count,), jnp.float32)
    key_rows, totals, positive = lax.fori_loop(
        0, cycle_size - 1, first_turn, (own_keys, start_zero, start_zero)
    )
    totals, positive = total_terms(
        key_rows, (cycle_index - (cycle_size - 1)) % cycle_size, totals, positive
    )

    def grad_terms(key_rows, owner_index, carried, grad_query):
        logits, matches = block_scores(queries, key_rows, owner_index, partner, factor)
        coeffs = (
            jnp.exp(logits - logit_scale) / totals[:, None] - matches.astype(jnp.float32)
        ).astype(jnp.bfloat16)
        grad_query = grad_query + factor * jnp.dot(
            coeffs, key_rows, preferred_element_type=jnp.float32
        )
        carried = carried + factor * lax.dot_general(
            coeffs, queries, (((0,), (0,)), ((), ())), preferred_element_type=jnp.float32
        )
        return (carried, grad_query)

    def second_turn(turn_index, loop_state):
        key_rows, carried, grad_query = loop_state
        owner_index = (cycle_index - turn_index) % cycle_size
        carried, grad_query = grad_terms(key_rows, owner_index, carried, grad_query)
        key_rows = passed_along(key_rows, "dp", 1)
        carried = passed_along(carried, "dp", 1)
        return (key_rows, carried, grad_query)

    start_grads = jnp.zeros(own_keys.shape, jnp.float32)
    key_rows, carried, grad_query = lax.fori_loop(
        0, cycle_size - 1, second_turn, (own_keys, start_grads, start_grads)
    )
    carried, grad_query = grad_terms(
        key_rows, (cycle_index - (cycle_size - 1)) % cycle_size, carried, grad_query
    )
    grad_key = passed_along(carried, "dp", 1)
    losses = logit_scale + jnp.log(totals) - positive
    grad_unit = jnp.concatenate([grad_query, grad_key], 0)
    grad_embed = inverse * (
        grad_unit - unit_rows * jnp.mean(unit_rows * grad_unit, 1, keepdims=True)
    )
    grad_embed_bf = grad_embed.astype(jnp.bfloat16)
    filter_rows = proj_weight.shape[0] // chan_count
    pooled_rows = lax.dynamic_slice_in_dim(pooled_bf, chan_index * filter_rows, filter_rows, 1)
    proj_terms = lax.dot_general(
        pooled_rows, grad_embed_bf, (((0,), (0,)), ((), ())), preferred_element_type=jnp.float32
    )
    grad_proj = lax.psum_scatter(proj_terms, "dp", scatter_dimension=1, tiled=True)
    grad_pool = lax.dot_general(
        grad_embed_bf, proj_weight, (((1,), (1,)), ((), ())), preferred_element_type=jnp.float32
    )
    grad_mixed = (grad_pool[:, :, None] / length * silu_slope(mixed)).astype(jnp.bfloat16)
    mix_terms = jnp.einsum("nft,nct->fc", grad_mixed, conv_time, preferred_element_type=jnp.float32)
    grad_conv = jnp.einsum(
        "fc,nft->nct", pw_weight, grad_mixed, preferred_element_type=jnp.float32
    ).astype(jnp.bfloat16)
    grad_pw = lax.psum(mix_terms, ("dp", "chan"))
    grad_local = lax.all_to_all(grad_conv, "chan", split_axis=1, concat_axis=2, tiled=True)
    extended = jnp.pad(stacked, ((0, 0), (0, 0), (rim_width, 0)))
    kernel_part = kernel_terms(grad_local, extended)
    grad_dw = lax.psum(kernel_part, "dp")
    return (losses, grad_dw, grad_pw, grad_proj)


def solution(mesh):
    placed = (P("dp", "chan", None), P("dp", "chan", None), P(), P(), P(), P("dp"))
    return jax.shard_map(
        body,
        mesh=mesh,
        in_specs=placed,
        out_specs=(P("dp"), P("chan", None), P(), P("chan", "dp")),
        check_vma=False,
    )
```

profile of v0, /device:TPU:2, one launch (start us, length us, event | category | flops | bytes accessed | tf_op | source)
XLA Modules:
  0.0 708.4 jit_solution(9025586352325555345)
XLA Ops:
  10.7 7.9 %copy.34 = bf16[32,8,4096]{0,1,2:T(8,128)(2,1)} copy(bf16[32,8,4096]{2,1,0:T(8,128)(2,1)S(1)} %constant_dynamic-update-slice_fusion) | data formatting | bytes 4194304 | tf_op jit(solution)/shard_map/concatenate | solution.py:58
  18.6 10.5 %slice.49 = f32[32,8,4080]{0,1,2:T(8,128)} slice(bf16[32,8,4096]{0,1,2:T(8,128)(2,1)} %copy.34), slice={[0:32], [0:8], [0:4080]} | slice | bytes 8355840 | tf_op jit(solution)/shard_map/slice | solution.py:24
  30.5 6.0 slice.50
  36.5 6.0 slice.51
  42.5 23.1 %fusion.44 = bf16[4096,8,32]{2,1,0:T(8,128)(2,1)} fusion(f32[32,8,4048]{0,1,2:T(8,128)} %slice.51, f32[8]{0:T(128)S(1)} %get-tuple-element.488, f32[32,8,4064]{0,1,2:T(8,128)} %slice.50, f32[8]{0:T(128)S(1)} %get-tuple-element.489, f32[32,8,4080]{0,1,2:T(8,128)} %slice.49, f32[8]{0:T(128)S(1)} %get-tuple-element.490, bf16[32,8,4096]{0,1,2:T(8,128)(2,1)} %copy.34, ...), kind=kLoop, calls=%fused_computation.88 | loop fusion | flops 9437184 | bytes 16679040
  65.6 14.5 %reshape.59 = bf16[16,2,32768]{2,1,0:T(2,128)(2,1)} reshape(bf16[4096,8,32]{2,1,0:T(8,128)(2,1)} %fusion.44) | data formatting | bytes 4194304
  80.1 11.3 %all-to-all-start = ((bf16[16,2,32768]{2,1,0:T(2,128)(2,1)}), bf16[16,2,32768]{2,1,0:T(2,128)(2,1)}, u32[]{:S(2)}, u32[]{:S(2)}) async-start(bf16[16,2,32768]{2,1,0:T(2,128)(2,1)} %reshape.59), calls=%async_computation | async-start | bytes 4194304 | tf_op jit(solution)/shard_map/all_to_all | solution.py:69
  91.4 50.5 %all-to-all-done = bf16[16,2,32768]{2,1,0:T(2,128)(2,1)} async-done(((bf16[16,2,32768]{2,1,0:T(2,128)(2,1)}), bf16[16,2,32768]{2,1,0:T(2,128)(2,1)}, u32[]{:S(2)}, u32[]{:S(2)}) %all-to-all-start) | async-done | bytes 2097184 | tf_op jit(solution)/shard_map/all_to_all | solution.py:69
  141.9 12.9 %reshape.60 = bf16[4096,8,32]{2,1,0:T(8,128)(2,1)} reshape(bf16[16,2,32768]{2,1,0:T(2,128)(2,1)} %all-to-all-done) | data formatting | bytes 4194304
  154.8 10.5 %copy.36 = bf16[32,16,8,256]{3,2,1,0:T(8,128)(2,1)} copy(bf16[32,16,8,256]{0,2,3,1:T(8,128)(2,1)} %bitcast.123) | data formatting | bytes 4194304 | tf_op jit(solution)/shard_map/all_to_all | solution.py:69
  165.3 6.2 fusion.12
  171.5 74.3 %psum.21 = bf16[32,256]{1,0:T(8,128)(2,1)S(1)} all-reduce(f32[32,256]{1,0:T(8,128)S(1)} %broadcast_multiply_fusion), channel_id=1, replica_groups=mesh['dp'=16,'chan'=16] {'chan'}, use_global_device_ids=true, to_apply=%region_1.2 | all-reduce | flops 8192 | bytes 49152 | tf_op jit(solution)/shard_map/psum | solution.py:73
  246.3 74.0 %while.40 = (s32[]{:T(128)}, bf16[16,1024]{1,0:T(8,128)(2,1)S(1)}, f32[16]{0:T(128)S(1)}, f32[16]{0:T(128)S(1)}, bf16[16,1024]{1,0:T(8,128)(2,1)S(1)}, /*index=5...) while((s32[]{:T(128)}, bf16[16,1024]{1,0:T(8,128)(2,1)S(1)}, ...), condition=%wide.region_6.7_spmd.clone, body=%wide.region_3.6_spmd.clone.sunk | while | flops 525888 | bytes 263144 | solution.py:97
  246.6 3.1 collective-permute-done
  249.9 3.2 collective-permute-done
  253.3 3.2 collective-permute-done
  256.6 3.6 collective-permute-done
  260.4 5.3 collective-permute-done
  265.9 5.3 collective-permute-done
  271.3 5.3 collective-permute-done
  276.8 5.3 collective-permute-done
  282.2 5.3 collective-permute-done
  287.7 5.3 collective-permute-done
  293.2 5.3 collective-permute-done
  298.6 5.3 collective-permute-done
  304.1 5.3 collective-permute-done
  309.5 5.3 collective-permute-done
  315.0 5.3 collective-permute-done
  320.9 92.6 %while.41 = (s32[]{:T(128)}, bf16[16,1024]{1,0:T(8,128)(2,1)S(1)}, f32[16,1024]{1,0:T(8,128)S(1)}, f32[16,1024]{1,0:T(8,128)S(1)}, bf16[16,1024]{1,0:T(8,128)(2,...) while((s32[]{:T(128)}, bf16[16,1024]{1,0:T(8,128)(2,1)S(1)}, ...), condition=%wide.region_10.11_spmd.clone, body=%wide.region_9.10_spmd.clone.sunk | while | flops 1656608 | bytes 854104 | solution.py:126
  321.6 4.9 collective-permute-done.1
  327.8 4.6 collective-permute-done.1
  335.7 2.9 collective-permute-done.1
  341.9 2.9 collective-permute-done.1
  348.1 2.9 collective-permute-done.1
  354.2 2.9 collective-permute-done.1
  360.4 2.9 collective-permute-done.1
  366.6 2.9 collective-permute-done.1
  372.8 2.9 collective-permute-done.1
  379.0 2.9 collective-permute-done.1
  385.2 2.9 collective-permute-done.1
  414.2 5.6 collective-permute-done.3
  420.4 5.0 fusion.16
  430.0 4.6 copy.39
  434.6 4.4 all-to-all-start.1
  440.3 4.8 fusion.25
  445.1 64.7 %reduce-scatter.4.cloned.1.call-done = f32[64,16]{1,0:T(8,128)} async-done(((f32[1024,16]{1,0:T(8,128)}), f32[64,16]{1,0:T(8,128)}) %reduce-scatter.4.cloned.1.call-update) | async-done | bytes 4112
  516.8 28.9 %psum.22 = f32[8,4]{0,1:T(4,128)} all-reduce(f32[8,4]{0,1:T(4,128)S(1)} %pad_maximum_fusion.1), channel_id=1, replica_groups=mesh['dp'=16,'chan'=16] {'dp'}, use_global_device_ids=true, to_apply=%region_12.13 | all-reduce | flops 32 | bytes 256 | tf_op jit(solution)/shard_map/psum | solution.py:157
  545.7 153.7 %all-reduce.6.cloned.1.call-done = f32[256,128]{1,0:T(8,128)} async-done(((f32[256,128]{1,0:T(8,128)}), f32[256,128]{1,0:T(8,128)}) %all-reduce.6.cloned.1.call-update) | async-done | bytes 131088 | tf_op jit(solution)/shard_map/psum | solution.py:153
  (248 shorter events, 80.5 us)
Async XLA Ops:
  80.1 61.8 %all-to-all-start = ((bf16[16,2,32768]{2,1,0:T(2,128)(2,1)}), bf16[16,2,32768]{2,1,0:T(2,128)(2,1)}, u32[]{:S(2)}, u32[]{:S(2)}) async-start(bf16[16,2,32768]{2,1,0:T(2,128)(2,1)} %reshape.59), calls=%async_computation | async-start | bytes 4194304 | tf_op jit(solution)/shard_map/all_to_all | solution.py:69
  246.3 3.4 collective-permute-start
  256.4 3.8 collective-permute-start
  260.2 5.4 collective-permute-start
  265.7 5.4 collective-permute-start
  271.2 5.4 collective-permute-start
  276.6 5.4 collective-permute-start
  282.1 5.4 collective-permute-start
  287.5 5.4 collective-permute-start
  293.0 5.4 collective-permute-start
  298.4 5.4 collective-permute-start
  303.9 5.4 collective-permute-start
  309.3 5.4 collective-permute-start
  314.8 5.4 collective-permute-start
  320.9 5.5 collective-permute-start.1
  321.4 5.9 collective-permute-start.2
  327.2 5.1 collective-permute-start.1
  327.6 5.6 collective-permute-start.2
  333.1 5.4 collective-permute-start.1
  333.4 5.9 collective-permute-start.2
  339.3 5.4 collective-permute-start.1
  339.6 5.9 collective-permute-start.2
  345.5 5.4 collective-permute-start.1
  345.8 5.9 collective-permute-start.2
  351.7 5.4 collective-permute-start.1
  352.0 5.9 collective-permute-start.2
  357.9 5.4 collective-permute-start.1
  358.2 5.9 collective-permute-start.2
  364.0 5.4 collective-permute-start.1
  364.4 5.9 collective-permute-start.2
  370.2 5.4 collective-permute-start.1
  370.5 5.9 collective-permute-start.2
  376.4 5.4 collective-permute-start.1
  376.7 5.9 collective-permute-start.2
  382.6 5.4 collective-permute-start.1
  382.9 5.9 collective-permute-start.2
  388.8 5.4 collective-permute-start.1
  389.1 5.9 collective-permute-start.2
  395.0 5.4 collective-permute-start.1
  395.3 5.9 collective-permute-start.2
  401.1 5.4 collective-permute-start.1
  401.5 5.9 collective-permute-start.2
  407.3 5.4 collective-permute-start.1
  407.7 5.9 collective-permute-start.2
  413.8 6.1 collective-permute-start.3
  434.6 76.7 %all-to-all-start.1 = ((bf16[32,128,256]{2,0,1:T(8,128)(2,1)}), bf16[32,128,256]{2,0,1:T(8,128)(2,1)}, u32[]{:S(2)}, u32[]{:S(2)}) async-start(bf16[32,128,256]{2,0,1:T(8,128)(2,1)} %copy.39), calls=%async_computation.1 | async-start | bytes 4194304 | tf_op jit(solution)/shard_map/all_to_all | solution.py:154
  439.0 70.8 %reduce-scatter.4.cloned.1.call-start = ((), (), s32[]{:S(2)}) async-start(), calls=%async_computation.4 | async-start | bytes 557056
  440.2 259.2 %all-reduce.6.cloned.1.call-start = ((), (), s32[]{:S(2)}) async-start(), calls=%async_computation.3 | async-start | bytes 262144 | tf_op jit(solution)/shard_map/psum | solution.py:153
  (8 other events, 419.2 us)
Sparse Core Ops, SparseCore 0:
  442.3 67.4 reduce-scatter.3
Sparse Core Ops, SparseCore 1:
  446.8 252.6 all-reduce.5
where the time goes:
time: 710 us; the launch traced here: 708 us
  waiting for transfers between devices  403 us (57%)
  blocking collectives  103 us (15%)
  local copies, waits for them, and re-layouts  84.8 us (12%)
  starting transfers between devices  43.8 us (6%)
  other arithmetic  32.1 us (5%)
  matrix products  24.8 us (3%)
  between operations  15.7 us (2%)
    psum x1, waiting for transfers between devices, body(): grad_pw = lax.psum(mix_terms, ('dp', 'chan'))  154 us
    ppermute x46, waiting for transfers between devices, passed_along(): return lax.ppermute(value, axis, pairs)  135 us
    psum x1, blocking collectives, body(): pooled = lax.psum(partial_pool, 'chan')  74.3 us
    unnamed x3, waiting for transfers between devices  64.7 us
    all_to_all x1, waiting for transfers between devices, body(): lax.all_to_all(conv_local, 'chan', split_axis=2, concat_axis=1, tiled=True)  50.5 us
    unnamed x18, local copies, waits for them, and re-layouts  35.1 us
    psum x1, blocking collectives, body(): grad_dw = lax.psum(kernel_part, 'dp')  28.9 us
    ppermute x46, starting transfers between devices, passed_along(): return lax.ppermute(value, axis, pairs)  28.1 us
  transfers between devices with their start and end apart: 50, of which 49 were waited for; matrix products, arithmetic and copies ran while one was open for 3% of the time, Pallas kernels for 0%

commit v1 on v0

--- a/solution.py
+++ b/solution.py
@@ -66,7 +66,15 @@
     local_metrics = anchors.shape[1]
     local_kernel = lax.dynamic_slice_in_dim(dw_weight, chan_index * local_metrics, local_metrics, 0)
     conv_local = depthwise(stacked, local_kernel)
-    conv_rows = lax.all_to_all(conv_local, "chan", split_axis=2, concat_axis=1, tiled=True)
+    conv_rows = jnp.concatenate(
+        jax.lax.all_to_all(
+            jnp.stack(jnp.split(conv_local, jax.lax.axis_size("chan"), axis=2), axis=0),
+            axis_name="chan",
+            split_axis=0,
+            concat_axis=0,
+        ),
+        axis=1,
+    )
     mixed = jnp.einsum("fc,nct->nft", pw_weight, conv_rows, preferred_element_type=jnp.float32)
     partial_pool = jnp.sum(jax.nn.silu(mixed), 2) / length
     conv_time, mixed, partial_pool = (conv_rows, mixed, partial_pool)

time: 710 us -> 640 us (0.901)
  local copies, waits for them, and re-layouts: 84.8 us -> 32.2 us
  other arithmetic: 32.1 us -> 15.4 us
    unnamed x4 -> x3, other arithmetic: 23.1 us -> 0.01 us
    unnamed x18 -> x31, local copies, waits for them, and re-layouts: 35.1 us -> 16.5 us
    slice x3, local copies, waits for them, and re-layouts: 22.4 us -> 7.36 us  [depthwise(): widened[:, :, :length - offset_steps]]
    all_to_all x1 -> x0, local copies, waits for them, and re-layouts: 10.5 us -> none  [body(): lax.all_to_all(conv_local, 'chan', split_axis=2, concat_axis=1, tiled=True)]
    concatenate x2 -> x1, local copies, waits for them, and re-layouts: 9.23 us -> 0.07 us  [body(): stacked = jnp.concatenate([anchors, views], 0)]
where the time goes in v1:
time: 640 us; the launch traced here: 639 us
  waiting for transfers between devices  404 us (63%)
  blocking collectives  103 us (16%)
  starting transfers between devices  44 us (7%)
  local copies, waits for them, and re-layouts  32.2 us (5%)
  matrix products  24.9 us (4%)
  between operations  15.7 us (2%)
  other arithmetic  15.4 us (2%)
    psum x1, waiting for transfers between devices, body(): grad_pw = lax.psum(mix_terms, ('dp', 'chan'))  154 us
    ppermute x46, waiting for transfers between devices, passed_along(): return lax.ppermute(value, axis, pairs)  135 us
    psum x1, blocking collectives, body(): pooled = lax.psum(partial_pool, 'chan')  74.3 us
    unnamed x3, waiting for transfers between devices  64.7 us
    all_to_all x1, waiting for transfers between devices, body(): jax.lax.all_to_all(jnp.stack(jnp.split(conv_local, jax.lax.axis_size('cha...  50.5 us
    psum x1, blocking collectives, body(): grad_dw = lax.psum(kernel_part, 'dp')  28.9 us
    ppermute x46, starting transfers between devices, passed_along(): return lax.ppermute(value, axis, pairs)  28.1 us
    unnamed x31, local copies, waits for them, and re-layouts  16.5 us
  transfers between devices with their start and end apart: 50, of which 49 were waited for; matrix products, arithmetic and copies ran while one was open for 3% of the time, Pallas kernels for 0%

profile of v1, /device:TPU:2, one launch (start us, length us, event | category | flops | bytes accessed | tf_op | source)
XLA Modules:
  0.0 639.4 jit_solution(2513624307807100844)
XLA Ops:
  17.1 6.4 add_convert_fusion
  34.2 11.4 %all-to-all-start = ((bf16[16,32,8,256]{3,2,1,0:T(8,128)(2,1)}), bf16[16,32,8,256]{3,2,1,0:T(8,128)(2,1)}, u32[]{:S(2)}, u32[]{:S(2)}) async-start(bf16[16,32,8,256]{3,2,1,0:T(8,128)(2,1)} %fusion.37), calls=%async_computation | async-start | bytes 4194304 | tf_op jit(solution)/shard_map/all_to_all | solution.py:70
  45.7 50.5 %all-to-all-done = bf16[16,32,8,256]{3,2,1,0:T(8,128)(2,1)} async-done(((bf16[16,32,8,256]{3,2,1,0:T(8,128)(2,1)}), bf16[16,32,8,256]{3,2,1,0:T(8,128)(2,1)}, u32[]{:S(2)}, u32[]{:S(2)}) %all-to-all-start) | async-done | bytes 2097184 | tf_op jit(solution)/shard_map/all_to_all | solution.py:70
  96.1 6.2 fusion.12
  102.3 74.3 %psum.21 = bf16[32,256]{1,0:T(8,128)(2,1)S(1)} all-reduce(f32[32,256]{1,0:T(8,128)S(1)} %broadcast_multiply_fusion), channel_id=1, replica_groups=mesh['dp'=16,'chan'=16] {'chan'}, use_global_device_ids=true, to_apply=%region_1.2 | all-reduce | flops 8192 | bytes 49152 | tf_op jit(solution)/shard_map/psum | solution.py:81
  177.1 74.0 %while.40 = (s32[]{:T(128)}, bf16[16,1024]{1,0:T(8,128)(2,1)S(1)}, f32[16]{0:T(128)S(1)}, f32[16]{0:T(128)S(1)}, bf16[16,1024]{1,0:T(8,128)(2,1)S(1)}, /*index=5...) while((s32[]{:T(128)}, bf16[16,1024]{1,0:T(8,128)(2,1)S(1)}, ...), condition=%wide.region_6.7_spmd.clone, body=%wide.region_3.6_spmd.clone.sunk | while | flops 525888 | bytes 263144 | solution.py:105
  177.4 3.1 collective-permute-done
  180.7 3.2 collective-permute-done
  184.1 3.2 collective-permute-done
  187.4 3.7 collective-permute-done
  191.3 5.3 collective-permute-done
  196.7 5.3 collective-permute-done
  202.2 5.3 collective-permute-done
  207.6 5.3 collective-permute-done
  213.1 5.3 collective-permute-done
  218.5 5.3 collective-permute-done
  224.0 5.3 collective-permute-done
  229.4 5.3 collective-permute-done
  234.9 5.3 collective-permute-done
  240.3 5.3 collective-permute-done
  245.8 5.3 collective-permute-done
  251.8 92.6 %while.41 = (s32[]{:T(128)}, bf16[16,1024]{1,0:T(8,128)(2,1)S(1)}, f32[16,1024]{1,0:T(8,128)S(1)}, f32[16,1024]{1,0:T(8,128)S(1)}, bf16[16,1024]{1,0:T(8,128)(2,...) while((s32[]{:T(128)}, bf16[16,1024]{1,0:T(8,128)(2,1)S(1)}, ...), condition=%wide.region_10.11_spmd.clone, body=%wide.region_9.10_spmd.clone.sunk | while | flops 1656608 | bytes 854104 | solution.py:134
  252.4 4.9 collective-permute-done.1
  258.6 4.6 collective-permute-done.1
  266.5 2.9 collective-permute-done.1
  272.7 2.9 collective-permute-done.1
  278.9 2.9 collective-permute-done.1
  285.1 2.9 collective-permute-done.1
  291.3 2.9 collective-permute-done.1
  297.4 2.9 collective-permute-done.1
  303.6 2.9 collective-permute-done.1
  309.8 2.9 collective-permute-done.1
  316.0 2.9 collective-permute-done.1
  322.2 2.9 collective-permute-done.1
  328.4 2.9 collective-permute-done.1
  334.5 2.9 collective-permute-done.1
  340.7 2.9 collective-permute-done.1
  345.1 5.6 collective-permute-done.3
  351.2 5.0 fusion.16
  358.2 2.6 convert_bitcast_fusion
  360.8 4.6 copy.36
  365.4 4.4 all-to-all-start.1
  371.1 4.8 fusion.27
  375.9 64.7 %reduce-scatter.4.cloned.1.call-done = f32[64,16]{1,0:T(8,128)} async-done(((f32[1024,16]{1,0:T(8,128)}), f32[64,16]{1,0:T(8,128)}) %reduce-scatter.4.cloned.1.call-update) | async-done | bytes 4112
  442.0 2.8 copy.37
  444.8 2.8 fusion.17
  447.6 28.9 %psum.22 = f32[8,4]{0,1:T(4,128)} all-reduce(f32[8,4]{0,1:T(4,128)S(1)} %pad_maximum_fusion.1), channel_id=1, replica_groups=mesh['dp'=16,'chan'=16] {'dp'}, use_global_device_ids=true, to_apply=%region_12.13 | all-reduce | flops 32 | bytes 256 | tf_op jit(solution)/shard_map/psum | solution.py:165
  476.5 153.8 %all-reduce.6.cloned.1.call-done = f32[256,128]{1,0:T(8,128)} async-done(((f32[256,128]{1,0:T(8,128)}), f32[256,128]{1,0:T(8,128)}) %all-reduce.6.cloned.1.call-update) | async-done | bytes 131088 | tf_op jit(solution)/shard_map/psum | solution.py:161
  (260 shorter events, 76.5 us)
Async XLA Ops:
  34.2 61.9 %all-to-all-start = ((bf16[16,32,8,256]{3,2,1,0:T(8,128)(2,1)}), bf16[16,32,8,256]{3,2,1,0:T(8,128)(2,1)}, u32[]{:S(2)}, u32[]{:S(2)}) async-start(bf16[16,32,8,256]{3,2,1,0:T(8,128)(2,1)} %fusion.37), calls=%async_computation | async-start | bytes 4194304 | tf_op jit(solution)/shard_map/all_to_all | solution.py:70
  177.1 3.4 collective-permute-start
  187.2 3.8 collective-permute-start
  191.1 5.4 collective-permute-start
  196.5 5.4 collective-permute-start
  202.0 5.4 collective-permute-start
  207.4 5.4 collective-permute-start
  212.9 5.4 collective-permute-start
  218.3 5.4 collective-permute-start
  223.8 5.4 collective-permute-start
  229.3 5.4 collective-permute-start
  234.7 5.4 collective-permute-start
  240.2 5.4 collective-permute-start
  245.6 5.4 collective-permute-start
  251.8 5.5 collective-permute-start.1
  252.2 5.9 collective-permute-start.2
  258.1 5.1 collective-permute-start.1
  258.4 5.6 collective-permute-start.2
  263.9 5.4 collective-permute-start.1
  264.3 5.9 collective-permute-start.2
  270.1 5.4 collective-permute-start.1
  270.4 5.9 collective-permute-start.2
  276.3 5.4 collective-permute-start.1
  276.6 5.9 collective-permute-start.2
  282.5 5.4 collective-permute-start.1
  282.8 5.9 collective-permute-start.2
  288.7 5.4 collective-permute-start.1
  289.0 5.9 collective-permute-start.2
  294.9 5.4 collective-permute-start.1
  295.2 5.9 collective-permute-start.2
  301.0 5.4 collective-permute-start.1
  301.4 5.9 collective-permute-start.2
  307.2 5.4 collective-permute-start.1
  307.6 5.9 collective-permute-start.2
  313.4 5.4 collective-permute-start.1
  313.7 5.9 collective-permute-start.2
  319.6 5.4 collective-permute-start.1
  319.9 5.9 collective-permute-start.2
  325.8 5.4 collective-permute-start.1
  326.1 5.9 collective-permute-start.2
  332.0 5.4 collective-permute-start.1
  332.3 5.9 collective-permute-start.2
  338.2 5.4 collective-permute-start.1
  338.5 5.9 collective-permute-start.2
  344.6 6.1 collective-permute-start.3
  365.4 76.6 %all-to-all-start.1 = ((bf16[32,128,256]{2,0,1:T(8,128)(2,1)}), bf16[32,128,256]{2,0,1:T(8,128)(2,1)}, u32[]{:S(2)}, u32[]{:S(2)}) async-start(bf16[32,128,256]{2,0,1:T(8,128)(2,1)} %copy.36), calls=%async_computation.1 | async-start | bytes 4194304 | tf_op jit(solution)/shard_map/all_to_all | solution.py:162
  369.8 70.8 %reduce-scatter.4.cloned.1.call-start = ((), (), s32[]{:S(2)}) async-start(), calls=%async_computation.4 | async-start | bytes 557056
  371.0 259.3 %all-reduce.6.cloned.1.call-start = ((), (), s32[]{:S(2)}) async-start(), calls=%async_computation.3 | async-start | bytes 262144 | tf_op jit(solution)/shard_map/psum | solution.py:161
  (8 other events, 374.7 us)
Sparse Core Ops, SparseCore 0:
  373.2 67.3 reduce-scatter.3
Sparse Core Ops, SparseCore 1:
  377.6 252.7 all-reduce.5
